TPU v7x, 32 devices: a whole 2x2x4 slice. The times are simulated.
32 devices in a mesh: freq: 4 (over z), space: 8 (over y, x, core).
Axes of the slice: x: 2, y: 2, z: 4, core: 2. Of those that a mesh axis runs over, the one named last changes fastest.
Arguments:
- recorded: bfloat16 [8, 2, 2048, 128], P('freq', None, 'space'), may hold values from -6 to 6
- v_factors: bfloat16 [8, 8, 2, 2048, 128], P('freq', None, None, 'space'), may hold values from -0.25 to 0.25
- u_factors: bfloat16 [8, 2, 2048, 8, 128], P('freq', None, 'space'), may hold values from -0.25 to 0.25
- tile_ranks: int32 [8, 8, 8], P('freq'), may hold values from 0 to 128, as said below
- mute_start: int32 [2048, 128], P('space', 'freq'), may hold values from 0 to 127
Outputs:
- muted_traces: float32 [2048, 128, 128], P('space', 'freq')
Inputs may be any that keep to these rules, and one draw needn't show every extreme that they name: `tile_ranks`: entries with i equal to j are 128; every other entry is 0 or 64.
All inputs are finite; a program needn't handle non-finite values.
Results may differ from a plain program's by a relative error of at most 0.0041.
Values may be sent and summed in bfloat16 or wider, within the bound.
A program may use at most 64 MiB of HBM per device.

v0:
```python
import math

import jax
import jax.numpy as jnp
from jax import lax
from jax.sharding import PartitionSpec as P

NT = 128


def apply_rows(received, row_factors):
    freq_count = received.shape[0]
    merged = received.reshape(
        freq_count, received.shape[1] * received.shape[2], 2, received.shape[4]
    )
    products = jnp.einsum(
        "fcpm,fmbs->fcpbs", row_factors, merged, preferred_element_type=jnp.float32
    )
    real_part = products[:, 0, :, 0] - products[:, 1, :, 1]
    imag_part = products[:, 0, :, 1] + products[:, 1, :, 0]
    return jnp.stack([real_part, imag_part], axis=1)


def time_basis(count, freq_total):
    freq_index = lax.iota(jnp.int32, count)
    weights = 1 + freq_index * (NT // 2 // freq_total)
    times = lax.iota(jnp.int32, NT)
    phase = (weights[:, None] * times[None, :] % NT).astype(jnp.float32) * (2.0 * math.pi / NT)
    scale = 1.0 / math.sqrt(2.0 * freq_total)
    return (jnp.cos(phase) * scale, -jnp.sin(phase) * scale)


def to_time(spectra, cos_basis, sin_basis):
    spectra_float = spectra.astype(jnp.float32)
    high = lax.Precision.HIGHEST
    return jnp.einsum("fps,ft->pst", spectra_float[:, 0], cos_basis, precision=high) + jnp.einsum(
        "fps,ft->pst", spectra_float[:, 1], sin_basis, precision=high
    )


def gathered_time(spectra, freq_total):
    cos_basis, sin_basis = time_basis(freq_total, freq_total)
    return to_time(spectra, cos_basis, sin_basis)


def shards(recorded, v_factors, u_factors, tile_ranks, mute_start):
    freq_count = recorded.shape[0]
    tile_rows = recorded.shape[2]
    tile_count = lax.axis_size("space")
    rank_width = v_factors.shape[4]
    half_width = rank_width // 2
    freq_total = freq_count * lax.axis_size("freq")
    column = lax.axis_index("space")
    real_in = recorded[:, 0]
    imag_in = recorded[:, 1]
    upper_half = jnp.stack([real_in, imag_in], axis=2)
    lower_half = jnp.stack([-imag_in, real_in], axis=2)
    stacked = jnp.concatenate([upper_half, lower_half], axis=1)
    column_factors = v_factors.reshape(freq_count, tile_count, 2 * tile_rows, rank_width)
    column_ranks = lax.dynamic_index_in_dim(tile_ranks, column, 2, keepdims=False)
    rank_index = lax.iota(jnp.int32, rank_width)
    low_factors = column_factors[:, :, :, :half_width]
    send_blocks = jnp.einsum(
        "fiak,fabs->fikbs", low_factors, stacked, preferred_element_type=jnp.float32
    )
    kept = rank_index[None, None, :half_width] < column_ranks[:, :, None]
    send_blocks = jnp.where(kept[:, :, :, None, None], send_blocks, 0.0).astype(jnp.bfloat16)
    send_factors = u_factors[:, :, :, :, :half_width].reshape(
        freq_count, 2, tile_rows, tile_count * half_width
    )
    own_v = lax.dynamic_index_in_dim(v_factors, column, 1, keepdims=False)[:, :, :, half_width:]
    own_v = own_v.reshape(freq_count, 2 * tile_rows, rank_width - half_width)
    own_blocks = jnp.einsum("fak,fabs->fkbs", own_v, stacked, preferred_element_type=jnp.float32)
    own_rank = lax.dynamic_index_in_dim(column_ranks, column, 1, keepdims=False)
    own_kept = rank_index[None, half_width:] < own_rank[:, None]
    own_blocks = jnp.where(own_kept[:, :, None, None], own_blocks, 0.0).astype(jnp.bfloat16)
    own_u = lax.dynamic_index_in_dim(u_factors, column, 3, keepdims=False)[:, :, :, half_width:]
    extra = apply_rows(own_blocks[:, None], own_u)
    summed = apply_rows(
        lax.all_to_all(send_blocks, "space", split_axis=1, concat_axis=1, tiled=True),
        row_factors=send_factors,
    )
    spectra = (summed + extra).astype(jnp.bfloat16)
    traces = gathered_time(
        lax.all_to_all(spectra, "freq", split_axis=3, concat_axis=0, tiled=True),
        freq_total=freq_total,
    )
    times = lax.iota(jnp.int32, NT)
    return jnp.where(times[None, None, :] >= mute_start[:, :, None], traces, 0.0)


def solution(mesh):
    placed = (
        P("freq", None, "space", None),
        P("freq", None, None, "space", None),
        P("freq", None, "space", None, None),
        P("freq", None, None),
        P("space", "freq"),
    )
    return jax.shard_map(
        shards, mesh=mesh, in_specs=placed, out_specs=P("space", "freq", None), check_vma=False
    )
```

profile of v0, /device:TPU:0, one launch (start us, length us, event | category | flops | bytes accessed | tf_op | source)
XLA Modules:
  0.0 45.6 jit_solution(9611368856776564932)
XLA Ops:
  0.0 0.0 copy-start
  0.0 0.0 copy-start.1
  0.0 1.1 %fusion.46 = bf16[2,256,1,128]{3,1,2,0:T(8,128)(2,1)S(1)} fusion(bf16[2,2,256,128]{3,2,1,0:T(8,128)(2,1)} %param.5), kind=kLoop, calls=%fused_computation.72 | loop fusion | flops 65536 | bytes 262144 | tf_op jit(solution)/shard_map/neg | solution.py:57
  1.1 1.0 %slice_bitcast_fusion.15 = (bf16[2,256,1,128]{3,1,2,0:T(8,128)(2,1)S(1)}, bf16[2,256,1,128]{3,1,2,0:T(8,128)(2,1)S(1)}) fusion(bf16[2,2,256,128]{3,2,1,0:T(8,128)(2,1)} %param.5), kind=kLoop, calls=%fused_computation.33 | loop fusion | bytes 524288 | tf_op jit(solution)/shard_map/stack;squeeze | solution.py:56
  2.1 0.0 copy-start.2
  2.1 0.0 copy-start.3
  2.1 0.0 copy-done
  2.1 0.2 dynamic-slice_reduce_fusion
  2.3 0.1 broadcast_compare_fusion
  2.4 2.4 %fusion.3 = bf16[2,8,64,2,128]{4,2,1,3,0:T(8,128)(2,1)S(1)} fusion(bf16[2,8,512,128]{3,2,1,0:T(8,128)(2,1)} %bitcast.106, pred[2,8,64]{2,1,0:T(8,128)(4,1)S(1)} %broadcast_compare_fusion, bf16[2,256,1,128]{3,1,2,0:T(8,128)(2,1)S(1)} %get-tuple-element.8, bf16[2,256,1,128]{3,1,2,0:T(8,128)(2,1)S(1)} %fusion.46, bf16[2,256,1,128]{3,1,2,0:T(8,128)(2,1)S(1)} %get-tuple-element.7), kind=kOutput, calls=%fused_computation.7 | convolution fusion | flops 271056896 | bytes 3015680 | tf_op jit(solution)/shard_map/fiak,fabs->fikbs/dot_general | solution.py:63
  4.8 0.8 %copy.54 = bf16[2,8,64,2,128]{4,2,3,0,1:T(8,128)(2,1)} copy(bf16[2,8,64,2,128]{4,2,1,3,0:T(8,128)(2,1)S(1)} %fusion.3) | data formatting | bytes 1048576 | tf_op jit(solution)/shard_map/convert_element_type | solution.py:67
  5.6 5.2 %all-to-all-start = ((bf16[2,8,64,2,128]{4,2,3,0,1:T(8,128)(2,1)}), bf16[2,8,64,2,128]{4,2,3,0,1:T(8,128)(2,1)}, u32[]{:S(2)}, u32[]{:S(2)}) async-start(bf16[2,8,64,2,128]{4,2,3,0,1:T(8,128)(2,1)} %copy.54), calls=%async_computation | async-start | bytes 1048576 | tf_op jit(solution)/shard_map/all_to_all | solution.py:80
  10.8 0.2 dynamic-slice_reduce_fusion.1
  11.0 0.0 copy-done.2
  11.1 0.0 copy-done.3
  11.1 0.1 slice.64
  11.1 0.0 copy-done.1
  11.1 0.5 %constant_dynamic-slice_fusion = bf16[2,2,256,1,128]{4,3,2,1,0:T(2,128)(2,1)S(1)} fusion(bf16[2,2,256,8,128]{4,3,2,1,0:T(8,128)(2,1)S(1)} %copy-done.1, s32[]{:T(128)S(6)} %select_n.34), kind=kLoop, calls=%fused_computation.59 | loop fusion | bytes 524292 | tf_op jit(solution)/shard_map/jit(dynamic_index_in_dim)/dynamic_slice | solution.py:77
  11.7 0.1 broadcast_compare_fusion.1
  11.8 1.0 %dynamic-slice_bitcast_fusion = bf16[2,2,256,128]{3,2,1,0:T(8,128)(2,1)S(1)} fusion(bf16[2,8,2,256,128]{4,3,2,1,0:T(8,128)(2,1)} %param.6, s32[]{:T(128)S(6)} %select_n.34), kind=kLoop, calls=%fused_computation.26 | loop fusion | bytes 524292 | tf_op jit(solution)/shard_map/jit(dynamic_index_in_dim)/squeeze | solution.py:71
  12.7 0.8 %slice.78 = bf16[2,2,256,64]{3,2,1,0:T(8,128)(2,1)} slice(bf16[2,2,256,128]{3,2,1,0:T(8,128)(2,1)S(1)} %dynamic-slice_bitcast_fusion), slice={[0:2], [0:2], [0:256], [64:128]} | slice | bytes 262144 | tf_op jit(solution)/shard_map/slice | solution.py:71
  13.6 0.3 copy.61
  13.9 1.2 %copy.90 = bf16[2,2,256,8,64]{2,4,3,1,0:T(8,128)(2,1)S(1)} copy(bf16[2,2,256,8,64]{4,3,2,1,0:T(8,128)(2,1)S(1)} %bitcast.100) | data formatting | bytes 2097152
  15.1 1.4 %fusion.5 = bf16[2,64,2,128,1]{3,1,2,0,4:T(8,128)(2,1)S(1)} fusion(bf16[2,512,64,1]{2,1,3,0:T(8,128)(2,1)} %bitcast.105, bf16[2,256,1,128]{3,1,2,0:T(8,128)(2,1)} %copy-done.3, bf16[2,256,1,128]{3,1,2,0:T(8,128)(2,1)S(1)} %fusion.46, bf16[2,256,1,128]{3,1,2,0:T(8,128)(2,1)} %copy-done.2, pred[2,64]{1,0:T(4,128)(4,1)S(1)} %broadcast_compare_fusion.1), kind=kOutput, calls=%fused_computation.10 | convolution fusion | flops 35717120 | bytes 589952 | tf_op jit(solution)/shard_map/fak,fabs->fkbs/dot_general | solution.py:73
  16.4 0.3 fusion.14
  16.8 3.9 %all-to-all-done = bf16[2,8,64,2,128]{4,2,3,0,1:T(8,128)(2,1)} async-done(((bf16[2,8,64,2,128]{4,2,3,0,1:T(8,128)(2,1)}), bf16[2,8,64,2,128]{4,2,3,0,1:T(8,128)(2,1)}, u32[]{:S(2)}, u32[]{:S(2)}) %all-to-all-start) | async-done | bytes 524320 | tf_op jit(solution)/shard_map/all_to_all | solution.py:80
  20.7 1.1 %copy.55 = bf16[2,8,64,2,128]{4,2,1,3,0:T(8,128)(2,1)S(1)} copy(bf16[2,8,64,2,128]{4,2,3,0,1:T(8,128)(2,1)} %all-to-all-done) | data formatting | bytes 1048576 | tf_op jit(solution)/shard_map/all_to_all | solution.py:80
  21.7 0.5 %convolution_bitcast_fusion = f32[2,2,256,2,128]{2,4,1,3,0:T(8,128)S(1)} fusion(bf16[2,512,2,128,1]{3,1,4,2,0:T(8,128)(2,1)S(1)} %bitcast.101, bf16[2,2,256,512,1]{2,3,1,4,0:T(8,128)(2,1)S(1)} %bitcast.99), kind=kOutput, calls=%fused_computation.5 | convolution fusion | flops 268435456 | bytes 2621440 | tf_op jit(solution)/shard_map/fcpm,fmbs->fcpbs/dot_general | solution.py:16
  22.3 0.1 fusion.9
  22.4 0.0 copy-start.4
  22.4 0.1 fusion.6
  22.5 1.0 %copy.68 = bf16[2,2,256,128]{2,0,1,3:T(2,128)(2,1)} copy(bf16[2,2,256,128]{2,3,0,1:T(8,128)(2,1)S(1)} %fusion.6) | data formatting | bytes 524288 | tf_op jit(solution)/shard_map/convert_element_type | solution.py:83
  23.5 5.2 %all-to-all-start.1 = ((bf16[2,2,256,128]{2,0,1,3:T(2,128)(2,1)}), bf16[2,2,256,128]{2,0,1,3:T(2,128)(2,1)S(1)}, u32[]{:S(2)}, u32[]{:S(2)}) async-start(bf16[2,2,256,128]{2,0,1,3:T(2,128)(2,1)} %copy.68), calls=%async_computation.1 | async-start | bytes 524288 | tf_op jit(solution)/shard_map/all_to_all | solution.py:85
  28.7 6.8 %all-to-all-done.1 = bf16[2,2,256,128]{2,0,1,3:T(2,128)(2,1)S(1)} async-done(((bf16[2,2,256,128]{2,0,1,3:T(2,128)(2,1)}), bf16[2,2,256,128]{2,0,1,3:T(2,128)(2,1)S(1)}, u32[]{:S(2)}, u32[]{:S(2)}) %all-to-all-start.1) | async-done | bytes 262176 | tf_op jit(solution)/shard_map/all_to_all | solution.py:85
  35.4 0.2 copy.99
  35.6 0.1 all_to_all.20
  35.7 2.4 %fusion.13 = f32[256,32,128]{2,0,1:T(8,128)S(1)} fusion(bf16[8,2,256,32]{2,0,3,1:T(8,128)(2,1)S(1)} %all_to_all.20, s32[8]{0:T(128)S(1)} %multiply_add_fusion), kind=kOutput, calls=%fused_computation.29 | convolution fusion | flops 100678656 | bytes 4325888 | tf_op jit(solution)/shard_map/fps,ft->pst/dot_general | solution.py:36
  38.1 0.0 copy-done.4
  38.1 3.1 %add_select_fusion = f32[256,32,128]{2,0,1:T(8,128)S(1)} fusion(f32[256,32,128]{2,0,1:T(8,128)S(1)} %fusion.13, s32[256,32]{0,1:T(8,128)S(1)} %copy-done.4, bf16[8,2,256,32]{2,0,3,1:T(8,128)(2,1)S(1)} %all_to_all.20, s32[8]{0:T(128)S(1)} %multiply_add_fusion), kind=kOutput, calls=%fused_computation | convolution fusion | flops 103825408 | bytes 8552960 | tf_op jit(solution)/shard_map/fps,ft->pst/dot_general | solution.py:36
  41.2 4.4 %copy.70 = f32[256,32,128]{2,1,0:T(8,128)} copy(f32[256,32,128]{2,0,1:T(8,128)S(1)} %add_select_fusion) | data formatting | bytes 8388608 | tf_op jit(solution)/shard_map/jit(_where)/select_n | solution.py:89
  (4 shorter events, 0.0 us)
Async XLA Ops:
  0.0 2.1 %copy-start = (s32[2,8,8]{2,1,0:T(8,128)S(1)}, s32[2,8,8]{2,1,0:T(8,128)}, u32[]{:S(2)}) copy-start(s32[2,8,8]{2,1,0:T(8,128)} %param.8) | copy-start | bytes 1540
  0.0 11.1 %copy-start.1 = (bf16[2,2,256,8,128]{4,3,2,1,0:T(8,128)(2,1)S(1)}, bf16[2,2,256,8,128]{4,3,2,1,0:T(8,128)(2,1)}, u32[]{:S(2)}) copy-start(bf16[2,2,256,8,128]{4,3,2,1,0:T(8,128)(2,1)} %param.7) | copy-start | bytes 6291460
  2.1 9.0 %copy-start.2 = (bf16[2,256,1,128]{3,1,2,0:T(8,128)(2,1)}, bf16[2,256,1,128]{3,1,2,0:T(8,128)(2,1)S(1)}, u32[]{:S(2)}) copy-start(bf16[2,256,1,128]{3,1,2,0:T(8,128)(2,1)S(1)} %get-tuple-element.7) | copy-start | bytes 393220
  2.1 9.0 %copy-start.3 = (bf16[2,256,1,128]{3,1,2,0:T(8,128)(2,1)}, bf16[2,256,1,128]{3,1,2,0:T(8,128)(2,1)S(1)}, u32[]{:S(2)}) copy-start(bf16[2,256,1,128]{3,1,2,0:T(8,128)(2,1)S(1)} %get-tuple-element.8) | copy-start | bytes 393220
  5.6 15.0 %all-to-all-start = ((bf16[2,8,64,2,128]{4,2,3,0,1:T(8,128)(2,1)}), bf16[2,8,64,2,128]{4,2,3,0,1:T(8,128)(2,1)}, u32[]{:S(2)}, u32[]{:S(2)}) async-start(bf16[2,8,64,2,128]{4,2,3,0,1:T(8,128)(2,1)} %copy.54), calls=%async_computation | async-start | bytes 1048576 | tf_op jit(solution)/shard_map/all_to_all | solution.py:80
  22.4 15.7 %copy-start.4 = (s32[256,32]{0,1:T(8,128)S(1)}, s32[256,32]{0,1:T(8,128)}, u32[]{:S(2)}) copy-start(s32[256,32]{0,1:T(8,128)} %param.9) | copy-start | bytes 98308
  23.5 12.0 %all-to-all-start.1 = ((bf16[2,2,256,128]{2,0,1,3:T(2,128)(2,1)}), bf16[2,2,256,128]{2,0,1,3:T(2,128)(2,1)S(1)}, u32[]{:S(2)}, u32[]{:S(2)}) async-start(bf16[2,2,256,128]{2,0,1,3:T(2,128)(2,1)} %copy.68), calls=%async_computation.1 | async-start | bytes 524288 | tf_op jit(solution)/shard_map/all_to_all | solution.py:85
where the time goes:
time: 46.1 us; the launch traced here: 45.6 us
  local copies, waits for them, and re-layouts  12.9 us (28%)
  waiting for transfers between devices  10.6 us (23%)
  starting transfers between devices  10.4 us (23%)
  matrix products  10 us (22%)
  other arithmetic  1.44 us (3%)
    all_to_all x1, waiting for transfers between devices, shards(): lax.all_to_all(spectra, 'freq', split_axis=3, concat_axis=0, tiled=True)  6.77 us
    all_to_all x1, starting transfers between devices, shards(): lax.all_to_all(spectra, 'freq', split_axis=3, concat_axis=0, tiled=True)  5.2 us
    all_to_all x1, starting transfers between devices, shards(): lax.all_to_all(send_blocks, 'space', split_axis=1, concat_axis=1, tiled=T...  5.2 us
    select_n x1, local copies, waits for them, and re-layouts, shards(): jnp.where(times[None, None, :] >= mute_start[:, :, None], traces, 0.0)  4.44 us
    all_to_all x1, waiting for transfers between devices, shards(): lax.all_to_all(send_blocks, 'space', split_axis=1, concat_axis=1, tiled=T...  3.86 us
    dot_general x1, matrix products, to_time(): jnp.einsum('fps,ft->pst', spectra_float[:, 1], sin_basis, precision=high)  3.06 us
    dot_general x1, matrix products, shards(): jnp.einsum('fiak,fabs->fikbs', low_factors, stacked, preferred_element_ty...  2.39 us
    dot_general x1, matrix products, to_time(): jnp.einsum('fps,ft->pst', spectra_float[:, 0], cos_basis, precision=high)  2.36 us
  transfers between devices with their start and end apart: 2, of which 2 were waited for; matrix products, arithmetic and copies ran while one was open for 13% of the time, Pallas kernels for 0%

commit v1 on v0

v1 whole, which is shorter than its diff:
```python
import functools
import math

import jax
import jax.numpy as jnp
import ml_dtypes
import numpy as np
from jax import lax
from jax.experimental import pallas as pl
from jax.experimental.pallas import tpu as pltpu
from jax.sharding import PartitionSpec as P

NT = 128
GROUP = 8
NT_DIMS = (((1,), (1,)), ((), ()))


def flipped(index, mask):
    result = index
    bit = 1
    while bit <= mask:
        if mask & bit:
            result = result + bit * (1 - 2 * ((index // bit) % 2))
        bit *= 2
    return result


def send_order(count):
    return sorted(range(count), key=lambda r: (-bin(r >> 1).count("1"), r % 2, r))


def spectra_kernel(
    tiles, parts, ranks_ref, recorded_ref, v_hbm, u_hbm, out_ref,
    v_ref, u_ref, wide_ref, data_ref, send_ref, recv_ref, own_ref, factor_ref, spec_ref,
    v_sems, u_sems, send_sems, recv_sems, zsend_sems, zrecv_sems,
):
    me = lax.axis_index("space")
    me_z = lax.axis_index("freq")
    freqs = recorded_ref.shape[0]
    tile = recorded_ref.shape[2]
    sources = recorded_ref.shape[3]
    ranks = v_ref.shape[3]
    half = ranks // 2
    share = sources // parts
    order = send_order(tiles)

    v_copies = [
        pltpu.make_async_copy(v_hbm.at[f], v_ref.at[f], v_sems.at[f]) for f in range(freqs)
    ]
    u_copies = [
        pltpu.make_async_copy(u_hbm.at[f], u_ref.at[f], u_sems.at[f]) for f in range(freqs)
    ]
    for f in range(freqs):
        v_copies[f].start()
    for f in range(freqs):
        u_copies[f].start()

    barrier = pltpu.get_barrier_semaphore()
    for r in range(1, tiles):
        pl.semaphore_signal(
            barrier, inc=1, device_id={"space": flipped(me, r)}, device_id_type=pl.DeviceIdType.MESH
        )
    for r in range(1, parts):
        pl.semaphore_signal(
            barrier, inc=1, device_id={"freq": lax.rem(me_z + r, parts)},
            device_id_type=pl.DeviceIdType.MESH,
        )

    def space_copy(f, r):
        return pltpu.make_async_remote_copy(
            src_ref=send_ref.at[f, r],
            dst_ref=recv_ref.at[f, me],
            send_sem=send_sems.at[f, r],
            recv_sem=recv_sems.at[f, r],
            device_id={"space": flipped(me, r)},
            device_id_type=pl.DeviceIdType.MESH,
        )

    def freq_copy(f, r):
        target = lax.rem(me_z + r, parts)
        return pltpu.make_async_remote_copy(
            src_ref=spec_ref.at[f, pl.ds(pl.multiple_of(target * share, share), share)],
            dst_ref=out_ref.at[me_z, f],
            send_sem=zsend_sems.at[f, r],
            recv_sem=zrecv_sems.at[f, r],
            device_id={"freq": target},
            device_id_type=pl.DeviceIdType.MESH,
        )

    for f in range(freqs):
        real = recorded_ref[f, 0].astype(jnp.float32).T.astype(jnp.bfloat16)
        imag = recorded_ref[f, 1].astype(jnp.float32).T.astype(jnp.bfloat16)
        data_ref[f, :sources, :tile] = real
        data_ref[f, :sources, tile:] = -imag
        data_ref[f, sources:, :tile] = imag
        data_ref[f, sources:, tile:] = real

    lane = lax.broadcasted_iota(jnp.int32, (sources, ranks), 1)
    low = lane < half
    for f in range(freqs):
        v_copies[f].wait()
        for r in order:
            row = flipped(me, r)
            blocks = jnp.dot(data_ref[f], v_ref[f, row], preferred_element_type=jnp.float32)
            kept = lane < ranks_ref[f, row, me]
            real = jnp.where(kept, blocks[:sources], 0.0)
            imag = jnp.where(kept, blocks[sources:], 0.0)
            packed = jnp.where(low, real, pltpu.roll(imag, half, 1)).astype(jnp.bfloat16)
            if r == 0:
                recv_ref[f, me] = packed
                own_ref[f] = jnp.where(low, pltpu.roll(real, half, 1), imag).astype(jnp.bfloat16)
            else:
                send_ref[f, r] = packed
                if f == 0 and r == order[0]:
                    pl.semaphore_wait(barrier, tiles - 1 + parts - 1)
                space_copy(f, r).start()

    wide_lane = lax.broadcasted_iota(jnp.int32, (tile, ranks), 1)
    wide_low = wide_lane < half
    for f in range(freqs):
        u_copies[f].wait()
        for c in range(2):
            wide_ref[c] = u_ref[f, c].astype(jnp.float32)
        for j in range(tiles + 1):
            start = j if j < tiles else me
            real = wide_ref[0, pl.ds(start, tile, stride=tiles), :]
            imag = wide_ref[1, pl.ds(start, tile, stride=tiles), :]
            real_roll = pltpu.roll(real, half, 1)
            imag_roll = pltpu.roll(imag, half, 1)
            if j < tiles:
                top = jnp.where(wide_low, real, -imag_roll)
                bottom = jnp.where(wide_low, imag, real_roll)
            else:
                top = jnp.where(wide_low, real_roll, -imag)
                bottom = jnp.where(wide_low, imag_roll, real)
            factor_ref[f, j, :tile] = top.astype(jnp.bfloat16)
            factor_ref[f, j, tile:] = bottom.astype(jnp.bfloat16)

    for f in range(freqs):
        total = lax.dot_general(
            own_ref[f], factor_ref[f, tiles], NT_DIMS, preferred_element_type=jnp.float32
        )
        for r in range(1, tiles):
            space_copy(f, r).wait_recv()
        for j in range(0, tiles, 2):
            lhs = jnp.concatenate([recv_ref[f, j], recv_ref[f, j + 1]], axis=1)
            rhs = jnp.concatenate([factor_ref[f, j], factor_ref[f, j + 1]], axis=1)
            total += lax.dot_general(lhs, rhs, NT_DIMS, preferred_element_type=jnp.float32)
        spec_ref[f] = total.astype(jnp.bfloat16)
        for r in range(1, parts):
            freq_copy(f, r).start()
        out_ref[me_z, f] = spec_ref[f, pl.ds(pl.multiple_of(me_z * share, share), share), :]

    for f in range(freqs):
        for r in range(1, tiles):
            space_copy(f, r).wait_send()
        for r in range(1, parts):
            freq_copy(f, r).wait_send()
            freq_copy(f, r).wait_recv()


def time_kernel(tile, spec_ref, mute_ref, basis_hbm, out_hbm, lhs_ref, basis_ref, rows_ref, basis_sem, out_sems):
    parts, freqs, share, _ = spec_ref.shape
    chunk = 64
    groups = share // GROUP
    basis_copy = pltpu.make_async_copy(basis_hbm, basis_ref, basis_sem)
    basis_copy.start()
    mute = mute_ref[...].T
    for side in range(tile // 128):
        for g in range(groups):
            pieces = []
            for z in range(parts):
                for f in range(freqs):
                    for c in range(2):
                        at = c * tile + side * 128
                        piece = spec_ref[z, f, :, at : at + 128].astype(jnp.float32)
                        pieces.append(piece[g * GROUP : (g + 1) * GROUP])
            block = jnp.concatenate(pieces, axis=0)
            lhs_ref[g, side * 128 : (side + 1) * 128, :] = block.T.astype(jnp.bfloat16)
    basis_copy.wait()
    times = lax.broadcasted_iota(jnp.int32, (chunk, NT), 1)
    copies = []
    for n in range(tile // chunk):
        lhs = jnp.concatenate([lhs_ref[g, n * chunk : (n + 1) * chunk, :] for g in range(groups)], axis=0)
        lhs = jnp.concatenate([lhs, lhs], axis=1)
        for pair in range(GROUP // 2):
            product = jnp.dot(
                lhs, basis_ref[:, pair * 2 * NT : (pair + 1) * 2 * NT], preferred_element_type=jnp.float32
            )
            for g in range(groups):
                for e in range(2):
                    s = g * GROUP + pair * 2 + e
                    values = product[g * chunk : (g + 1) * chunk, e * NT : (e + 1) * NT]
                    starts = mute[n * chunk : (n + 1) * chunk, s : s + 1]
                    rows_ref[pl.ds(n * chunk * share + s, chunk, stride=share), :] = jnp.where(
                        times >= starts, values, 0.0
                    )
        span = pl.ds(n * chunk * share, chunk * share)
        copy = pltpu.make_async_copy(rows_ref.at[span], out_hbm.at[span], out_sems.at[n])
        copy.start()
        copies.append(copy)
    for copy in copies:
        copy.wait()


def block_basis(freq_total):
    weights = 1 + np.arange(freq_total) * (NT // 2 // freq_total)
    phase = (weights[:, None] * np.arange(NT)[None, :] % NT) * (2.0 * math.pi / NT)
    scale = 1.0 / math.sqrt(2.0 * freq_total)
    table = np.stack([np.cos(phase) * scale, -np.sin(phase) * scale], axis=1)
    table = table.reshape(2 * freq_total, NT).astype(np.float32)
    high = table.astype(ml_dtypes.bfloat16)
    low = (table - high.astype(np.float32)).astype(ml_dtypes.bfloat16)
    both = np.stack([high, low])
    full = np.zeros((2, 2 * freq_total, GROUP, GROUP, NT), ml_dtypes.bfloat16)
    for g in range(GROUP):
        full[:, :, g, g, :] = both
    return full.reshape(4 * freq_total * GROUP, GROUP * NT)


def shards(tiles, parts, basis, recorded, v_factors, u_factors, tile_ranks, mute_start):
    freqs, _, tile, sources = recorded.shape
    ranks = v_factors.shape[4]
    share = sources // parts
    bf16 = jnp.bfloat16
    spectra = pl.pallas_call(
        functools.partial(spectra_kernel, tiles, parts),
        out_shape=jax.ShapeDtypeStruct((parts, freqs, share, 2 * tile), bf16),
        in_specs=[
            pl.BlockSpec(memory_space=pltpu.SMEM),
            pl.BlockSpec(memory_space=pltpu.VMEM),
            pl.BlockSpec(memory_space=pl.ANY),
            pl.BlockSpec(memory_space=pl.ANY),
        ],
        out_specs=pl.BlockSpec(memory_space=pltpu.VMEM),
        scratch_shapes=[
            pltpu.VMEM((freqs, tiles, 2 * tile, ranks), bf16),
            pltpu.VMEM((freqs, 2, tile * tiles, ranks), bf16),
            pltpu.VMEM((2, tile * tiles, ranks), jnp.float32),
            pltpu.VMEM((freqs, 2 * sources, 2 * tile), bf16),
            pltpu.VMEM((freqs, tiles, sources, ranks), bf16),
            pltpu.VMEM((freqs, tiles, sources, ranks), bf16),
            pltpu.VMEM((freqs, sources, ranks), bf16),
            pltpu.VMEM((freqs, tiles + 1, 2 * tile, ranks), bf16),
            pltpu.VMEM((freqs, sources, 2 * tile), bf16),
            pltpu.SemaphoreType.DMA((freqs,)),
            pltpu.SemaphoreType.DMA((freqs,)),
            pltpu.SemaphoreType.DMA((freqs, tiles)),
            pltpu.SemaphoreType.DMA((freqs, tiles)),
            pltpu.SemaphoreType.DMA((freqs, parts)),
            pltpu.SemaphoreType.DMA((freqs, parts)),
        ],
        compiler_params=pltpu.CompilerParams(collective_id=0, has_side_effects=True),
        name="spectra_kernel",
    )(
        tile_ranks,
        recorded,
        v_factors.reshape(freqs, tiles, 2 * tile, ranks),
        u_factors.reshape(freqs, 2, tile * tiles, ranks),
    )
    traces = pl.pallas_call(
        functools.partial(time_kernel, tile),
        out_shape=jax.ShapeDtypeStruct((tile * share, NT), jnp.float32),
        in_specs=[
            pl.BlockSpec(memory_space=pltpu.VMEM),
            pl.BlockSpec(memory_space=pltpu.VMEM),
            pl.BlockSpec(memory_space=pl.ANY),
        ],
        out_specs=pl.BlockSpec(memory_space=pl.ANY),
        scratch_shapes=[
            pltpu.VMEM((share // GROUP, tile, 128), bf16),
            pltpu.VMEM(basis.shape, bf16),
            pltpu.VMEM((tile * share, NT), jnp.float32),
            pltpu.SemaphoreType.DMA,
            pltpu.SemaphoreType.DMA((tile // 64,)),
        ],
        name="time_kernel",
    )(spectra, mute_start.T, jnp.asarray(basis))
    return traces.reshape(tile, share, NT)


def solution(mesh):
    placed = (
        P("freq", None, "space", None),
        P("freq", None, None, "space", None),
        P("freq", None, "space", None, None),
        P("freq", None, None),
        P("space", "freq"),
    )
    tiles, parts = mesh.shape["space"], mesh.shape["freq"]

    def run(*args):
        body = functools.partial(shards, tiles, parts, block_basis(args[0].shape[0]))
        return jax.shard_map(
            body, mesh=mesh, in_specs=placed, out_specs=P("space", "freq", None), check_vma=False
        )(*args)

    return run
```

time: 46.1 us -> 29 us (0.63)
  Pallas kernels: 0 us -> 28.8 us
  local copies, waits for them, and re-layouts: 12.9 us -> 0 us
  waiting for transfers between devices: 10.6 us -> 0 us
  starting transfers between devices: 10.4 us -> 0 us
  matrix products: 10 us -> 0 us
  other arithmetic: 1.44 us -> 0 us
    pallas_call x0 -> x2, Pallas kernels: none -> 28.8 us  [the longest x1 21.1 us: shards(): pl.pallas_call(functools.partial(spectra_kernel, tiles, parts), out_shape...]
    all_to_all x2 -> x0, waiting for transfers between devices: 10.6 us -> none  [the longest x1 6.77 us: shards(): lax.all_to_all(spectra, 'freq', split_axis=3, concat_axis=0, tiled=True)]
    all_to_all x2 -> x0, starting transfers between devices: 10.4 us -> none  [the longest x1 5.2 us: shards(): lax.all_to_all(spectra, 'freq', split_axis=3, concat_axis=0, tiled=True)]
    dot_general x6 -> x0, matrix products: 10 us -> none  [the longest x1 3.06 us: to_time(): jnp.einsum('fps,ft->pst', spectra_float[:, 1], sin_basis, precision=high)]
    select_n x1 -> x0, local copies, waits for them, and re-layouts: 4.44 us -> none  [shards(): jnp.where(times[None, None, :] >= mute_start[:, :, None], traces, 0.0)]
    convert_element_type x2 -> x0, local copies, waits for them, and re-layouts: 1.8 us -> none  [the longest x1 0.97 us: shards(): spectra = (summed + extra).astype(jnp.bfloat16)]
    all_to_all x3 -> x0, local copies, waits for them, and re-layouts: 1.36 us -> none  [the longest x1 1.08 us: shards(): lax.all_to_all(send_blocks, 'space', split_axis=1, concat_axis=1, tiled=T...]
    dynamic_slice x4 -> x0, local copies, waits for them, and re-layouts: 1.29 us -> none  [the longest x2 0.89 us: shards(): lax.dynamic_index_in_dim(u_factors, column, 3, keepdims=False)]
  transfers between devices with their start and end apart: 2 -> 0, of which waited for: 2 -> 0; matrix products, arithmetic and copies ran while one was open for 13% -> 0% of each run, Pallas kernels for 0% -> 0%
where the time goes in v1:
time: 29 us; the launch traced here: 28.8 us
  Pallas kernels  28.8 us (99%)
    pallas_call x1, Pallas kernels, shards(): pl.pallas_call(functools.partial(spectra_kernel, tiles, parts), out_shape...  21.1 us
    pallas_call x1, Pallas kernels, shards(): pl.pallas_call(functools.partial(time_kernel, tile), out_shape=jax.ShapeD...  7.71 us

profile of v1, /device:TPU:0, one launch (start us, length us, event | category | flops | bytes accessed | tf_op | source)
XLA Modules:
  0.0 28.8 jit_solution(3369701060778177613)
XLA Ops:
  0.0 21.1 %spectra_kernel.1.spec_ref = bf16[4,2,32,512]{3,2,1,0:T(8,128)(2,1)} custom-call(s32[2,8,8]{2,1,0:T(8,128)} %ranks_ref.1, bf16[2,2,256,128]{3,2,1,0:T(8,128)(2,1)} %recorded_ref.1, bf16[2,8,512,128]{3,2,1,0:T(8,128)(2,1)} %bitcast.4, bf16[2,2,2048,128]{3,2,1,0:T(8,128)(2,1)} %bitcast.5), custom_call_target="tpu_custom_call" | custom-call | tf_op jit(solution)/shard_map/spectra_kernel/pallas_call | solution.py:226
  21.1 7.7 %time_kernel.1 = f32[8192,128]{1,0:T(8,128)} custom-call(bf16[4,2,32,512]{3,2,1,0:T(8,128)(2,1)} %spectra_kernel.1.spec_ref, s32[32,256]{1,0:T(8,128)} %bitcast.6, bf16[256,1024]{1,0:T(8,128)(2,1)} %constant.2.clone.basis_hbm), custom_call_target="tpu_custom_call" | custom-call | tf_op jit(solution)/shard_map/time_kernel/pallas_call | solution.py:261

commit v2 on v1

--- a/solution.py
+++ b/solution.py
@@ -62,7 +62,7 @@
         )
     for r in range(1, parts):
         pl.semaphore_signal(
-            barrier, inc=1, device_id={"freq": lax.rem(me_z + r, parts)},
+            barrier, inc=1, device_id={"freq": flipped(me_z, r)},
             device_id_type=pl.DeviceIdType.MESH,
         )
 
@@ -77,9 +77,9 @@
         )
 
     def freq_copy(f, r):
-        target = lax.rem(me_z + r, parts)
+        target = flipped(me_z, r)
         return pltpu.make_async_remote_copy(
-            src_ref=spec_ref.at[f, pl.ds(pl.multiple_of(target * share, share), share)],
+            src_ref=spec_ref.at[f, target],
             dst_ref=out_ref.at[me_z, f],
             send_sem=zsend_sems.at[f, r],
             recv_sem=zrecv_sems.at[f, r],
@@ -97,23 +97,34 @@
 
     lane = lax.broadcasted_iota(jnp.int32, (sources, ranks), 1)
     low = lane < half
+    rank_of = lax.rem(lane, half)
     for f in range(freqs):
         v_copies[f].wait()
-        for r in order:
-            row = flipped(me, r)
-            blocks = jnp.dot(data_ref[f], v_ref[f, row], preferred_element_type=jnp.float32)
-            kept = lane < ranks_ref[f, row, me]
-            real = jnp.where(kept, blocks[:sources], 0.0)
-            imag = jnp.where(kept, blocks[sources:], 0.0)
-            packed = jnp.where(low, real, pltpu.roll(imag, half, 1)).astype(jnp.bfloat16)
-            if r == 0:
-                recv_ref[f, me] = packed
-                own_ref[f] = jnp.where(low, pltpu.roll(real, half, 1), imag).astype(jnp.bfloat16)
-            else:
-                send_ref[f, r] = packed
-                if f == 0 and r == order[0]:
-                    pl.semaphore_wait(barrier, tiles - 1 + parts - 1)
-                space_copy(f, r).start()
+        for first in range(0, tiles, 4):
+            group = order[first : first + 4]
+            rows = [flipped(me, r) for r in group]
+            packed_v = jnp.concatenate([v_ref[f, row, :, :half] for row in rows], axis=1)
+            blocks = jnp.dot(data_ref[f], packed_v, preferred_element_type=jnp.float32)
+            for n, (r, row) in enumerate(zip(group, rows)):
+                columns = slice((n // 2) * ranks, (n // 2 + 1) * ranks)
+                real, imag = blocks[:sources, columns], blocks[sources:, columns]
+                if n % 2 == 0:
+                    packed = jnp.where(low, real, pltpu.roll(imag, half, 1))
+                else:
+                    packed = jnp.where(low, pltpu.roll(real, half, 1), imag)
+                packed = jnp.where(rank_of < ranks_ref[f, row, me], packed, 0.0).astype(jnp.bfloat16)
+                if r == 0:
+                    recv_ref[f, me] = packed
+                else:
+                    send_ref[f, r] = packed
+                    if f == 0 and r == order[0]:
+                        pl.semaphore_wait(barrier, tiles - 1 + parts - 1)
+                    space_copy(f, r).start()
+    for f in range(freqs):
+        blocks = jnp.dot(data_ref[f], v_ref[f, me], preferred_element_type=jnp.float32)
+        packed = jnp.where(low, pltpu.roll(blocks[:sources], half, 1), blocks[sources:])
+        kept = rank_of + half < ranks_ref[f, me, me]
+        own_ref[f] = jnp.where(kept, packed, 0.0).astype(jnp.bfloat16)
 
     wide_lane = lax.broadcasted_iota(jnp.int32, (tile, ranks), 1)
     wide_low = wide_lane < half
@@ -136,20 +147,37 @@
             factor_ref[f, j, :tile] = top.astype(jnp.bfloat16)
             factor_ref[f, j, tile:] = bottom.astype(jnp.bfloat16)
 
+    rows = tile // parts
+    swap_lane = lax.broadcasted_iota(jnp.int32, (rows, sources), 1)
     for f in range(freqs):
         total = lax.dot_general(
-            own_ref[f], factor_ref[f, tiles], NT_DIMS, preferred_element_type=jnp.float32
+            factor_ref[f, tiles], own_ref[f], NT_DIMS, preferred_element_type=jnp.float32
         )
         for r in range(1, tiles):
             space_copy(f, r).wait_recv()
         for j in range(0, tiles, 2):
-            lhs = jnp.concatenate([recv_ref[f, j], recv_ref[f, j + 1]], axis=1)
-            rhs = jnp.concatenate([factor_ref[f, j], factor_ref[f, j + 1]], axis=1)
+            lhs = jnp.concatenate([factor_ref[f, j], factor_ref[f, j + 1]], axis=1)
+            rhs = jnp.concatenate([recv_ref[f, j], recv_ref[f, j + 1]], axis=1)
             total += lax.dot_general(lhs, rhs, NT_DIMS, preferred_element_type=jnp.float32)
-        spec_ref[f] = total.astype(jnp.bfloat16)
-        for r in range(1, parts):
+        for c in range(2):
+            pieces = [total[c * tile + q * rows : c * tile + (q + 1) * rows] for q in range(parts)]
+            bit = parts // 2
+            while bit >= 1:
+                width = bit * share
+                keep = lax.rem(swap_lane, 2 * width) < width
+                swapped = list(pieces)
+                for q in range(parts):
+                    if not q & bit:
+                        x, y = pieces[q], pieces[q + bit]
+                        swapped[q] = jnp.where(keep, x, pltpu.roll(y, width, 1))
+                        swapped[q + bit] = jnp.where(keep, pltpu.roll(x, sources - width, 1), y)
+                pieces = swapped
+                bit //= 2
+            for z in range(parts):
+                spec_ref[f, z, c * rows : (c + 1) * rows] = pieces[z].astype(jnp.bfloat16)
+        for r in range(parts - 1, 0, -1):
             freq_copy(f, r).start()
-        out_ref[me_z, f] = spec_ref[f, pl.ds(pl.multiple_of(me_z * share, share), share), :]
+        out_ref[me_z, f] = spec_ref[f, me_z]
 
     for f in range(freqs):
         for r in range(1, tiles):
@@ -159,46 +187,45 @@
             freq_copy(f, r).wait_recv()
 
 
-def time_kernel(tile, spec_ref, mute_ref, basis_hbm, out_hbm, lhs_ref, basis_ref, rows_ref, basis_sem, out_sems):
-    parts, freqs, share, _ = spec_ref.shape
-    chunk = 64
-    groups = share // GROUP
+def time_kernel(share, spec_ref, mute_ref, basis_hbm, out_hbm, basis_ref, rows_ref, basis_sem, out_sems):
+    parts, freqs, rows, sources = spec_ref.shape
+    rows //= 2
     basis_copy = pltpu.make_async_copy(basis_hbm, basis_ref, basis_sem)
     basis_copy.start()
-    mute = mute_ref[...].T
-    for side in range(tile // 128):
-        for g in range(groups):
+    times = lax.broadcasted_iota(jnp.int32, (share, NT), 1)
+    copies = []
+    for n in range(rows // (2 * GROUP)):
+        sides = []
+        for g in (2 * n, 2 * n + 1):
             pieces = []
             for z in range(parts):
                 for f in range(freqs):
                     for c in range(2):
-                        at = c * tile + side * 128
-                        piece = spec_ref[z, f, :, at : at + 128].astype(jnp.float32)
-                        pieces.append(piece[g * GROUP : (g + 1) * GROUP])
+                        at = c * rows + g * GROUP
+                        pieces.append(spec_ref[z, f, at : at + GROUP].astype(jnp.float32))
             block = jnp.concatenate(pieces, axis=0)
-            lhs_ref[g, side * 128 : (side + 1) * 128, :] = block.T.astype(jnp.bfloat16)
-    basis_copy.wait()
-    times = lax.broadcasted_iota(jnp.int32, (chunk, NT), 1)
-    copies = []
-    for n in range(tile // chunk):
-        lhs = jnp.concatenate([lhs_ref[g, n * chunk : (n + 1) * chunk, :] for g in range(groups)], axis=0)
+            sides.append(block.T.astype(jnp.bfloat16))
+        lhs = jnp.concatenate(sides, axis=0)
         lhs = jnp.concatenate([lhs, lhs], axis=1)
+        if n == 0:
+            basis_copy.wait()
         for pair in range(GROUP // 2):
             product = jnp.dot(
                 lhs, basis_ref[:, pair * 2 * NT : (pair + 1) * 2 * NT], preferred_element_type=jnp.float32
             )
-            for g in range(groups):
-                for e in range(2):
-                    s = g * GROUP + pair * 2 + e
-                    values = product[g * chunk : (g + 1) * chunk, e * NT : (e + 1) * NT]
-                    starts = mute[n * chunk : (n + 1) * chunk, s : s + 1]
-                    rows_ref[pl.ds(n * chunk * share + s, chunk, stride=share), :] = jnp.where(
-                        times >= starts, values, 0.0
-                    )
-        span = pl.ds(n * chunk * share, chunk * share)
-        copy = pltpu.make_async_copy(rows_ref.at[span], out_hbm.at[span], out_sems.at[n])
-        copy.start()
-        copies.append(copy)
+            for side in range(2):
+                for q in range(parts):
+                    for e in range(2):
+                        p = q * rows + (2 * n + side) * GROUP + pair * 2 + e
+                        at = side * sources + q * share
+                        values = product[at : at + share, e * NT : (e + 1) * NT]
+                        starts = mute_ref[:, p : p + 1]
+                        rows_ref[p * share : (p + 1) * share, :] = jnp.where(times >= starts, values, 0.0)
+        for q in range(parts):
+            span = pl.ds((q * rows + 2 * n * GROUP) * share, 2 * GROUP * share)
+            copy = pltpu.make_async_copy(rows_ref.at[span], out_hbm.at[span], out_sems.at[n, q])
+            copy.start()
+            copies.append(copy)
     for copy in copies:
         copy.wait()
 
@@ -225,7 +252,7 @@
     bf16 = jnp.bfloat16
     spectra = pl.pallas_call(
         functools.partial(spectra_kernel, tiles, parts),
-        out_shape=jax.ShapeDtypeStruct((parts, freqs, share, 2 * tile), bf16),
+        out_shape=jax.ShapeDtypeStruct((parts, freqs, 2 * tile // parts, sources), bf16),
         in_specs=[
             pl.BlockSpec(memory_space=pltpu.SMEM),
             pl.BlockSpec(memory_space=pltpu.VMEM),
@@ -242,7 +269,7 @@
             pltpu.VMEM((freqs, tiles, sources, ranks), bf16),
             pltpu.VMEM((freqs, sources, ranks), bf16),
             pltpu.VMEM((freqs, tiles + 1, 2 * tile, ranks), bf16),
-            pltpu.VMEM((freqs, sources, 2 * tile), bf16),
+            pltpu.VMEM((freqs, parts, 2 * tile // parts, sources), bf16),
             pltpu.SemaphoreType.DMA((freqs,)),
             pltpu.SemaphoreType.DMA((freqs,)),
             pltpu.SemaphoreType.DMA((freqs, tiles)),
@@ -259,7 +286,7 @@
         u_factors.reshape(freqs, 2, tile * tiles, ranks),
     )
     traces = pl.pallas_call(
-        functools.partial(time_kernel, tile),
+        functools.partial(time_kernel, share),
         out_shape=jax.ShapeDtypeStruct((tile * share, NT), jnp.float32),
         in_specs=[
             pl.BlockSpec(memory_space=pltpu.VMEM),
@@ -268,11 +295,10 @@
         ],
         out_specs=pl.BlockSpec(memory_space=pl.ANY),
         scratch_shapes=[
-            pltpu.VMEM((share // GROUP, tile, 128), bf16),
             pltpu.VMEM(basis.shape, bf16),
             pltpu.VMEM((tile * share, NT), jnp.float32),
             pltpu.SemaphoreType.DMA,
-            pltpu.SemaphoreType.DMA((tile // 64,)),
+            pltpu.SemaphoreType.DMA((tile // parts // (2 * GROUP), parts)),
         ],
         name="time_kernel",
     )(spectra, mute_start.T, jnp.asarray(basis))

time: 29 us -> 26.2 us (0.903)
  Pallas kernels: 28.8 us -> 26 us
    pallas_call x1, Pallas kernels: 7.71 us -> 4.81 us  [shards(): pl.pallas_call(functools.partial(time_kernel, share), out_shape=jax.Shape...]
where the time goes in v2:
time: 26.2 us; the launch traced here: 26 us
  Pallas kernels  26 us (99%)
    pallas_call x1, Pallas kernels, shards(): pl.pallas_call(functools.partial(spectra_kernel, tiles, parts), out_shape...  21.2 us
    pallas_call x1, Pallas kernels, shards(): pl.pallas_call(functools.partial(time_kernel, share), out_shape=jax.Shape...  4.81 us

profile of v2, /device:TPU:0, one launch (start us, length us, event | category | flops | bytes accessed | tf_op | source)
XLA Modules:
  0.0 26.0 jit_solution(18236637554528455547)
XLA Ops:
  0.0 21.2 %spectra_kernel.1.spec_ref = bf16[4,2,128,128]{3,2,1,0:T(8,128)(2,1)} custom-call(s32[2,8,8]{2,1,0:T(8,128)} %ranks_ref.1, bf16[2,2,256,128]{3,2,1,0:T(8,128)(2,1)} %recorded_ref.1, bf16[2,8,512,128]{3,2,1,0:T(8,128)(2,1)} %bitcast.4, bf16[2,2,2048,128]{3,2,1,0:T(8,128)(2,1)} %bitcast.5), custom_call_target="tpu_custom_call" | custom-call | tf_op jit(solution)/shard_map/spectra_kernel/pallas_call | solution.py:253
  21.2 4.8 %time_kernel.1 = f32[8192,128]{1,0:T(8,128)} custom-call(bf16[4,2,128,128]{3,2,1,0:T(8,128)(2,1)} %spectra_kernel.1.spec_ref, s32[32,256]{1,0:T(8,128)} %bitcast.6, bf16[256,1024]{1,0:T(8,128)(2,1)} %constant.2.clone.basis_hbm), custom_call_target="tpu_custom_call" | custom-call | tf_op jit(solution)/shard_map/time_kernel/pallas_call | solution.py:288

commit v3 on v2

--- a/solution.py
+++ b/solution.py
@@ -30,9 +30,10 @@
 
 
 def spectra_kernel(
-    tiles, parts, ranks_ref, recorded_ref, v_hbm, u_hbm, out_ref,
-    v_ref, u_ref, wide_ref, data_ref, send_ref, recv_ref, own_ref, factor_ref, spec_ref,
+    tiles, parts, ranks_hbm, recorded_hbm, v_hbm, u_hbm, mute_hbm, out_hbm, mask_hbm,
+    ranks_ref, recorded_ref, mute_ref, mask_ref, v_ref, u_ref, wide_ref, data_ref, send_ref, recv_ref, own_ref, factor_ref, spec_ref,
     v_sems, u_sems, send_sems, recv_sems, zsend_sems, zrecv_sems,
+    keep_sems, first_sems, mask_sems,
 ):
     me = lax.axis_index("space")
     me_z = lax.axis_index("freq")
@@ -50,10 +51,14 @@
     u_copies = [
         pltpu.make_async_copy(u_hbm.at[f], u_ref.at[f], u_sems.at[f]) for f in range(freqs)
     ]
-    for f in range(freqs):
-        v_copies[f].start()
-    for f in range(freqs):
-        u_copies[f].start()
+    ranks_copy = pltpu.make_async_copy(ranks_hbm, ranks_ref, first_sems.at[0])
+    data_copy = pltpu.make_async_copy(recorded_hbm, recorded_ref, first_sems.at[1])
+    mute_copy = pltpu.make_async_copy(mute_hbm, mute_ref, first_sems.at[2])
+    data_copy.start()
+    ranks_copy.start()
+    for copy in v_copies + u_copies:
+        copy.start()
+    mute_copy.start()
 
     barrier = pltpu.get_barrier_semaphore()
     for r in range(1, tiles):
@@ -76,17 +81,27 @@
             device_id_type=pl.DeviceIdType.MESH,
         )
 
-    def freq_copy(f, r):
+    rows = tile // parts
+
+    def freq_copy(f, c, r):
         target = flipped(me_z, r)
         return pltpu.make_async_remote_copy(
-            src_ref=spec_ref.at[f, target],
-            dst_ref=out_ref.at[me_z, f],
-            send_sem=zsend_sems.at[f, r],
-            recv_sem=zrecv_sems.at[f, r],
+            src_ref=spec_ref.at[f, target, pl.ds(c * rows, rows)],
+            dst_ref=out_hbm.at[me_z, f, pl.ds(c * rows, rows)],
+            send_sem=zsend_sems.at[f, c, r],
+            recv_sem=zrecv_sems.at[f, c, r],
             device_id={"freq": target},
             device_id_type=pl.DeviceIdType.MESH,
         )
 
+    def keep_copy(f, c):
+        return pltpu.make_async_copy(
+            spec_ref.at[f, me_z, pl.ds(c * rows, rows)],
+            out_hbm.at[me_z, f, pl.ds(c * rows, rows)],
+            keep_sems.at[f, c],
+        )
+
+    data_copy.wait()
     for f in range(freqs):
         real = recorded_ref[f, 0].astype(jnp.float32).T.astype(jnp.bfloat16)
         imag = recorded_ref[f, 1].astype(jnp.float32).T.astype(jnp.bfloat16)
@@ -98,14 +113,15 @@
     lane = lax.broadcasted_iota(jnp.int32, (sources, ranks), 1)
     low = lane < half
     rank_of = lax.rem(lane, half)
+    ranks_copy.wait()
     for f in range(freqs):
         v_copies[f].wait()
         for first in range(0, tiles, 4):
             group = order[first : first + 4]
-            rows = [flipped(me, r) for r in group]
-            packed_v = jnp.concatenate([v_ref[f, row, :, :half] for row in rows], axis=1)
+            targets = [flipped(me, r) for r in group]
+            packed_v = jnp.concatenate([v_ref[f, row, :, :half] for row in targets], axis=1)
             blocks = jnp.dot(data_ref[f], packed_v, preferred_element_type=jnp.float32)
-            for n, (r, row) in enumerate(zip(group, rows)):
+            for n, (r, row) in enumerate(zip(group, targets)):
                 columns = slice((n // 2) * ranks, (n // 2 + 1) * ranks)
                 real, imag = blocks[:sources, columns], blocks[sources:, columns]
                 if n % 2 == 0:
@@ -147,17 +163,18 @@
             factor_ref[f, j, :tile] = top.astype(jnp.bfloat16)
             factor_ref[f, j, tile:] = bottom.astype(jnp.bfloat16)
 
-    rows = tile // parts
     swap_lane = lax.broadcasted_iota(jnp.int32, (rows, sources), 1)
     for f in range(freqs):
         total = lax.dot_general(
             factor_ref[f, tiles], own_ref[f], NT_DIMS, preferred_element_type=jnp.float32
         )
-        for r in range(1, tiles):
-            space_copy(f, r).wait_recv()
-        for j in range(0, tiles, 2):
-            lhs = jnp.concatenate([factor_ref[f, j], factor_ref[f, j + 1]], axis=1)
-            rhs = jnp.concatenate([recv_ref[f, j], recv_ref[f, j + 1]], axis=1)
+        for first in [0] + list(range(2, tiles, 2))[::-1]:
+            pair = [flipped(me, first), flipped(me, first + 1)]
+            for r in (first, first + 1):
+                if r > 0:
+                    space_copy(f, r).wait_recv()
+            lhs = jnp.concatenate([factor_ref[f, j] for j in pair], axis=1)
+            rhs = jnp.concatenate([recv_ref[f, j] for j in pair], axis=1)
             total += lax.dot_general(lhs, rhs, NT_DIMS, preferred_element_type=jnp.float32)
         for c in range(2):
             pieces = [total[c * tile + q * rows : c * tile + (q + 1) * rows] for q in range(parts)]
@@ -175,24 +192,54 @@
                 bit //= 2
             for z in range(parts):
                 spec_ref[f, z, c * rows : (c + 1) * rows] = pieces[z].astype(jnp.bfloat16)
-        for r in range(parts - 1, 0, -1):
-            freq_copy(f, r).start()
-        out_ref[me_z, f] = spec_ref[f, me_z]
-
+            for r in range(parts - 1, 0, -1):
+                freq_copy(f, c, r).start()
+            keep_copy(f, c).start()
+
+    mute_copy.wait()
+    times = lax.broadcasted_iota(jnp.int32, (share, NT), 1)
+    span = 2 * GROUP
+    mask_copies = []
+    for n in range(rows // span):
+        for q in range(parts):
+            for i in range(span):
+                p = q * rows + n * span + i
+                at = (q * span + i) * share
+                starts = mute_ref[:, p : p + 1]
+                mask_ref[n, at : at + share] = jnp.where(times >= starts, 1.0, 0.0).astype(jnp.bfloat16)
+        copy = pltpu.make_async_copy(mask_ref.at[n], mask_hbm.at[n], mask_sems.at[n])
+        copy.start()
+        mask_copies.append(copy)
+
+    for copy in mask_copies:
+        copy.wait()
     for f in range(freqs):
         for r in range(1, tiles):
             space_copy(f, r).wait_send()
-        for r in range(1, parts):
-            freq_copy(f, r).wait_send()
-            freq_copy(f, r).wait_recv()
-
-
-def time_kernel(share, spec_ref, mute_ref, basis_hbm, out_hbm, basis_ref, rows_ref, basis_sem, out_sems):
+        for c in range(2):
+            keep_copy(f, c).wait()
+            for r in range(1, parts):
+                freq_copy(f, c, r).wait_send()
+                freq_copy(f, c, r).wait_recv()
+
+
+def time_kernel(
+    share, spec_hbm, mask_hbm, basis_hbm, out_hbm,
+    spec_ref, mask_ref, basis_ref, rows_ref, in_sems, mask_sems, out_sems,
+):
     parts, freqs, rows, sources = spec_ref.shape
     rows //= 2
-    basis_copy = pltpu.make_async_copy(basis_hbm, basis_ref, basis_sem)
+    spec_copy = pltpu.make_async_copy(spec_hbm, spec_ref, in_sems.at[0])
+    spec_copy.start()
+    basis_copy = pltpu.make_async_copy(basis_hbm, basis_ref, in_sems.at[1])
     basis_copy.start()
-    times = lax.broadcasted_iota(jnp.int32, (share, NT), 1)
+    mask_copies = [
+        pltpu.make_async_copy(mask_hbm.at[n], mask_ref.at[n], mask_sems.at[n])
+        for n in range(mask_ref.shape[0])
+    ]
+    for copy in mask_copies:
+        copy.start()
+    spec_copy.wait()
     copies = []
     for n in range(rows // (2 * GROUP)):
         sides = []
@@ -209,6 +256,7 @@
         lhs = jnp.concatenate([lhs, lhs], axis=1)
         if n == 0:
             basis_copy.wait()
+        mask_copies[n].wait()
         for pair in range(GROUP // 2):
             product = jnp.dot(
                 lhs, basis_ref[:, pair * 2 * NT : (pair + 1) * 2 * NT], preferred_element_type=jnp.float32
@@ -219,8 +267,9 @@
                         p = q * rows + (2 * n + side) * GROUP + pair * 2 + e
                         at = side * sources + q * share
                         values = product[at : at + share, e * NT : (e + 1) * NT]
-                        starts = mute_ref[:, p : p + 1]
-                        rows_ref[p * share : (p + 1) * share, :] = jnp.where(times >= starts, values, 0.0)
+                        row = (q * 2 * GROUP + side * GROUP + pair * 2 + e) * share
+                        mask = mask_ref[n, row : row + share].astype(jnp.float32)
+                        rows_ref[p * share : (p + 1) * share, :] = values * mask
         for q in range(parts):
             span = pl.ds((q * rows + 2 * n * GROUP) * share, 2 * GROUP * share)
             copy = pltpu.make_async_copy(rows_ref.at[span], out_hbm.at[span], out_sems.at[n, q])
@@ -250,17 +299,20 @@
     ranks = v_factors.shape[4]
     share = sources // parts
     bf16 = jnp.bfloat16
-    spectra = pl.pallas_call(
+    spec_shape = (parts, freqs, 2 * tile // parts, sources)
+    chunks = tile // parts // (2 * GROUP)
+    mask_shape = (chunks, tile * share // chunks, NT)
+    anywhere = pl.BlockSpec(memory_space=pl.ANY)
+    spectra, mask = pl.pallas_call(
         functools.partial(spectra_kernel, tiles, parts),
-        out_shape=jax.ShapeDtypeStruct((parts, freqs, 2 * tile // parts, sources), bf16),
-        in_specs=[
-            pl.BlockSpec(memory_space=pltpu.SMEM),
-            pl.BlockSpec(memory_space=pltpu.VMEM),
-            pl.BlockSpec(memory_space=pl.ANY),
-            pl.BlockSpec(memory_space=pl.ANY),
-        ],
-        out_specs=pl.BlockSpec(memory_space=pltpu.VMEM),
+        out_shape=(jax.ShapeDtypeStruct(spec_shape, bf16), jax.ShapeDtypeStruct(mask_shape, bf16)),
+        in_specs=[anywhere] * 5,
+        out_specs=(anywhere, anywhere),
         scratch_shapes=[
+            pltpu.SMEM(tile_ranks.shape, jnp.int32),
+            pltpu.VMEM(recorded.shape, bf16),
+            pltpu.VMEM((share, tile), jnp.int32),
+            pltpu.VMEM(mask_shape, bf16),
             pltpu.VMEM((freqs, tiles, 2 * tile, ranks), bf16),
             pltpu.VMEM((freqs, 2, tile * tiles, ranks), bf16),
             pltpu.VMEM((2, tile * tiles, ranks), jnp.float32),
@@ -274,8 +326,11 @@
             pltpu.SemaphoreType.DMA((freqs,)),
             pltpu.SemaphoreType.DMA((freqs, tiles)),
             pltpu.SemaphoreType.DMA((freqs, tiles)),
-            pltpu.SemaphoreType.DMA((freqs, parts)),
-            pltpu.SemaphoreType.DMA((freqs, parts)),
+            pltpu.SemaphoreType.DMA((freqs, 2, parts)),
+            pltpu.SemaphoreType.DMA((freqs, 2, parts)),
+            pltpu.SemaphoreType.DMA((freqs, 2)),
+            pltpu.SemaphoreType.DMA((3,)),
+            pltpu.SemaphoreType.DMA((chunks,)),
         ],
         compiler_params=pltpu.CompilerParams(collective_id=0, has_side_effects=True),
         name="spectra_kernel",
@@ -284,24 +339,24 @@
         recorded,
         v_factors.reshape(freqs, tiles, 2 * tile, ranks),
         u_factors.reshape(freqs, 2, tile * tiles, ranks),
+        mute_start.T,
     )
     traces = pl.pallas_call(
         functools.partial(time_kernel, share),
         out_shape=jax.ShapeDtypeStruct((tile * share, NT), jnp.float32),
-        in_specs=[
-            pl.BlockSpec(memory_space=pltpu.VMEM),
-            pl.BlockSpec(memory_space=pltpu.VMEM),
-            pl.BlockSpec(memory_space=pl.ANY),
-        ],
-        out_specs=pl.BlockSpec(memory_space=pl.ANY),
+        in_specs=[anywhere] * 3,
+        out_specs=anywhere,
         scratch_shapes=[
+            pltpu.VMEM(spec_shape, bf16),
+            pltpu.VMEM(mask_shape, bf16),
             pltpu.VMEM(basis.shape, bf16),
             pltpu.VMEM((tile * share, NT), jnp.float32),
-            pltpu.SemaphoreType.DMA,
-            pltpu.SemaphoreType.DMA((tile // parts // (2 * GROUP), parts)),
+            pltpu.SemaphoreType.DMA((2,)),
+            pltpu.SemaphoreType.DMA((chunks,)),
+            pltpu.SemaphoreType.DMA((chunks, parts)),
         ],
         name="time_kernel",
-    )(spectra, mute_start.T, jnp.asarray(basis))
+    )(spectra, mask, jnp.asarray(basis))
     return traces.reshape(tile, share, NT)
 
 

time: 26.2 us -> 23.9 us (0.912)
  Pallas kernels: 26 us -> 23.7 us
    pallas_call x1, Pallas kernels: 21.2 us -> 19.6 us  [shards(): pl.pallas_call(functools.partial(spectra_kernel, tiles, parts), out_shape...]
    pallas_call x1, Pallas kernels: 4.81 us -> 4.09 us  [shards(): pl.pallas_call(functools.partial(time_kernel, share), out_shape=jax.Shape...]
where the time goes in v3:
time: 23.9 us; the launch traced here: 23.7 us
  Pallas kernels  23.7 us (99%)
    pallas_call x1, Pallas kernels, shards(): pl.pallas_call(functools.partial(spectra_kernel, tiles, parts), out_shape...  19.6 us
    pallas_call x1, Pallas kernels, shards(): pl.pallas_call(functools.partial(time_kernel, share), out_shape=jax.Shape...  4.09 us

profile of v3, /device:TPU:0, one launch (start us, length us, event | category | flops | bytes accessed | tf_op | source)
XLA Modules:
  0.0 23.7 jit_solution(16106123389440117485)
XLA Ops:
  0.0 19.6 %spectra_kernel.1 = (bf16[4,2,128,128]{3,2,1,0:T(8,128)(2,1)}, bf16[4,2048,128]{2,1,0:T(8,128)(2,1)}) custom-call(s32[2,8,8]{2,1,0:T(8,128)} %ranks_hbm.1, bf16[2,2,256,128]{3,2,1,0:T(8,128)(2,1)} %recorded_hbm.1, bf16[2,8,512,128]{3,2,1,0:T(8,128)(2,1)} %bitcast.4, bf16[2,2,2048,128]{3,2,1,0:T(8,128)(2,1)} %bitcast.5, s32[32,256]{1,0:T(8,128)} %bitcast.6), custom_call_target="tpu_custom_call" | custom-call | tf_op jit(solution)/shard_map/spectra_kernel/pallas_call | solution.py:306
  19.6 4.1 %time_kernel.1 = f32[8192,128]{1,0:T(8,128)} custom-call(bf16[4,2,128,128]{3,2,1,0:T(8,128)(2,1)} %get-tuple-element.7.spec_hbm, bf16[4,2048,128]{2,1,0:T(8,128)(2,1)} %get-tuple-element.8.mask_hbm, bf16[256,1024]{1,0:T(8,128)(2,1)} %constant.2.clone.basis_hbm), custom_call_target="tpu_custom_call" | custom-call | tf_op jit(solution)/shard_map/time_kernel/pallas_call | solution.py:344

commit v4 on v3

--- a/solution.py
+++ b/solution.py
@@ -102,6 +102,10 @@
         )
 
     data_copy.wait()
+    lane = lax.broadcasted_iota(jnp.int32, (sources, ranks), 1)
+    low = lane < half
+    rank_of = lax.rem(lane, half)
+    ranks_copy.wait()
     for f in range(freqs):
         real = recorded_ref[f, 0].astype(jnp.float32).T.astype(jnp.bfloat16)
         imag = recorded_ref[f, 1].astype(jnp.float32).T.astype(jnp.bfloat16)
@@ -109,12 +113,6 @@
         data_ref[f, :sources, tile:] = -imag
         data_ref[f, sources:, :tile] = imag
         data_ref[f, sources:, tile:] = real
-
-    lane = lax.broadcasted_iota(jnp.int32, (sources, ranks), 1)
-    low = lane < half
-    rank_of = lax.rem(lane, half)
-    ranks_copy.wait()
-    for f in range(freqs):
         v_copies[f].wait()
         for first in range(0, tiles, 4):
             group = order[first : first + 4]
@@ -144,7 +142,7 @@
 
     wide_lane = lax.broadcasted_iota(jnp.int32, (tile, ranks), 1)
     wide_low = wide_lane < half
-    for f in range(freqs):
+    def prepare(f):
         u_copies[f].wait()
         for c in range(2):
             wide_ref[c] = u_ref[f, c].astype(jnp.float32)
@@ -165,6 +163,7 @@
 
     swap_lane = lax.broadcasted_iota(jnp.int32, (rows, sources), 1)
     for f in range(freqs):
+        prepare(f)
         total = lax.dot_general(
             factor_ref[f, tiles], own_ref[f], NT_DIMS, preferred_element_type=jnp.float32
         )

time: 23.9 us -> 23.8 us (level)
  no operation moved by 1% of the time
where the time goes in v4:
time: 23.8 us; the launch traced here: 23.7 us
  Pallas kernels  23.7 us (100%)
    pallas_call x1, Pallas kernels, shards(): pl.pallas_call(functools.partial(spectra_kernel, tiles, parts), out_shape...  19.6 us
    pallas_call x1, Pallas kernels, shards(): pl.pallas_call(functools.partial(time_kernel, share), out_shape=jax.Shape...  4.09 us

profile of v4, /device:TPU:0, one launch (start us, length us, event | category | flops | bytes accessed | tf_op | source)
XLA Modules:
  0.0 23.7 jit_solution(4706877015651739836)
XLA Ops:
  0.0 19.6 %spectra_kernel.1 = (bf16[4,2,128,128]{3,2,1,0:T(8,128)(2,1)}, bf16[4,2048,128]{2,1,0:T(8,128)(2,1)}) custom-call(s32[2,8,8]{2,1,0:T(8,128)} %ranks_hbm.1, bf16[2,2,256,128]{3,2,1,0:T(8,128)(2,1)} %recorded_hbm.1, bf16[2,8,512,128]{3,2,1,0:T(8,128)(2,1)} %bitcast.4, bf16[2,2,2048,128]{3,2,1,0:T(8,128)(2,1)} %bitcast.5, s32[32,256]{1,0:T(8,128)} %bitcast.6), custom_call_target="tpu_custom_call" | custom-call | tf_op jit(solution)/shard_map/spectra_kernel/pallas_call | solution.py:305
  19.6 4.1 %time_kernel.1 = f32[8192,128]{1,0:T(8,128)} custom-call(bf16[4,2,128,128]{3,2,1,0:T(8,128)(2,1)} %get-tuple-element.7.spec_hbm, bf16[4,2048,128]{2,1,0:T(8,128)(2,1)} %get-tuple-element.8.mask_hbm, bf16[256,1024]{1,0:T(8,128)(2,1)} %constant.2.clone.basis_hbm), custom_call_target="tpu_custom_call" | custom-call | tf_op jit(solution)/shard_map/time_kernel/pallas_call | solution.py:343
